TPU v7x, 256 devices: a whole 4x4x8 slice. The times are simulated.
256 devices in a mesh: blk: 8 (over z), lat: 4 (over x), depth: 8 (over y, core).
Axes of the slice: x: 4, y: 4, z: 8, core: 2. Of those that a mesh axis runs over, the one named last changes fastest.
Arguments:
- face_len: int32 [8, 4, 8, 6], P('blk', 'lat', 'depth'), may hold values from 0 to 128, as said below
- residual: float32 [8, 4, 8, 768, 512], P('blk', 'lat', 'depth'), as said below
- prev_direction: float32 [8, 4, 8, 768, 512], P('blk', 'lat', 'depth'), as said below
- prev_rho: float32 [512], replicated, may hold values from 0.5 to 4
- schur: float32 [8, 4, 8, 768, 768], P('blk', 'lat', 'depth'), as said below
- neumann: float32 [8, 4, 8, 768, 768], P('blk', 'lat', 'depth'), as said below
- coarse_basis: float32 [8, 4, 8, 768, 256], P('blk', 'lat', 'depth'), may hold values from -0.21875 to 0.21875
- coarse_inverse: float32 [8, 4, 8, 256, 256], P('blk', 'lat', 'depth'), as said below
- prim_owner: int32 [8, 4, 8, 256, 1], P('blk', 'lat', 'depth'), may hold values from 0 to 31; in each aligned block of 256 rows (0 to 255, 256 to 511, ..., all dimensions but the last counted through in order) at most 24 rows name the same one
- coarse_row: int32 [8, 4, 8, 256], P('blk', 'lat', 'depth'), may hold values from 0 to 255
Outputs:
- new_residual: float32 [8, 4, 8, 768, 512], P('blk', 'lat', 'depth')
- direction: float32 [8, 4, 8, 768, 512], P('blk', 'lat', 'depth')
- rho_now: float32 [512], replicated
- step_alpha: float32 [512], replicated
- res_norm: float32 [512], replicated
Inputs may be any that keep to these rules, and one draw needn't show every extreme that they name: `face_len`: two subdomains that share a face have equal lengths on it; faces on the outer ends of lat and depth have length 0. `residual`: the two copies of a shared interface row are equal, and rows past a face's length are zero. `prev_direction`: the two copies of a shared interface row are equal, and rows past a face's length are zero. `schur`: each matrix has a positive definite symmetric part. `neumann`: each matrix has a positive definite symmetric part. `coarse_inverse`: each matrix has a positive definite symmetric part. `prim_owner`: at most 24 primal dofs of one subdomain have the same owner.
All inputs are finite; a program needn't handle non-finite values.
Results may differ from a plain program's by a relative error of at most 0.00005.
Values sent between devices are 32-bit elements; how exact they have to be, the bound alone decides.
A program may use at most 64 MiB of HBM per device.

v0:
```python
import jax
import jax.numpy as jnp
from jax import lax
from jax.sharding import PartitionSpec as P

CAP = 24
exact_mode = lax.Precision.HIGHEST


def from_behind(x, axis, by):
    devices = lax.axis_size(axis)
    return lax.ppermute(x, axis, [(i, (i + by) % devices) for i in range(devices)])


def passed_along(block, axis, distance):
    devices = range(lax.axis_size(axis))
    route = [(i - distance, i) for i in devices if i - distance in devices]
    return lax.ppermute(block, axis, route)


def product(left, right):
    return jnp.dot(left, right, precision=exact_mode, preferred_element_type=jnp.float32)


def product_t(left, right):
    return lax.dot_general(
        left,
        right,
        (((0,), (0,)), ((), ())),
        precision=exact_mode,
        preferred_element_type=jnp.float32,
    )


def assemble(vector, live_mask):
    col_count = vector.shape[1]
    face_rows = vector.shape[0] // 6
    face_list = vector.reshape(6, face_rows, col_count)
    received = [None] * 6
    for facing in range(2):
        shift_by = 1 - 2 * facing
        received[facing] = from_behind(face_list[1 - facing], "blk", shift_by)
        received[2 + facing] = passed_along(face_list[3 - facing], "lat", shift_by)
        received[4 + facing] = passed_along(face_list[5 - facing], "depth", shift_by)
    return live_mask * (vector + jnp.stack(received).reshape(vector.shape))


def coarse_level(coarse_terms, owner_ids, row_ids, inverse):
    primal, col_count = coarse_terms.shape
    owners = lax.axis_size(("blk", "lat"))
    slots = owners * CAP
    owner_hit = (owner_ids[:, None] == lax.broadcasted_iota(jnp.int32, (primal, owners), 1)).astype(
        jnp.int32
    )
    owner_rank = jnp.sum(jnp.cumsum(owner_hit, axis=0) * owner_hit, axis=1) - 1
    slot_index = owner_ids * CAP + owner_rank
    packer = slot_index[None, :] == lax.broadcasted_iota(jnp.int32, (slots, primal), 0)
    pack_table = packer.astype(jnp.float32)
    outgoing = product(pack_table, coarse_terms).reshape(owners, CAP, col_count)
    outgoing_rows = (jnp.sum(jnp.where(packer, row_ids[None, :] + 1, 0), axis=1) - 1).reshape(
        owners, CAP
    )
    incoming, incoming_rows = (
        lax.all_to_all(outgoing, ("blk", "lat"), split_axis=0, concat_axis=0, tiled=True),
        lax.all_to_all(outgoing_rows, ("blk", "lat"), split_axis=0, concat_axis=0, tiled=True),
    )
    owned_rows = inverse.shape[0]
    picker = (
        incoming_rows.reshape(1, slots) == lax.broadcasted_iota(jnp.int32, (owned_rows, slots), 0)
    ).astype(jnp.float32)
    gathered = product(picker, incoming.reshape(slots, col_count))
    solved = product(inverse, gathered)
    answers = product_t(picker, solved)
    returned = lax.all_to_all(
        answers.reshape(owners, CAP, col_count),
        ("blk", "lat"),
        split_axis=0,
        concat_axis=0,
        tiled=True,
    )
    return product_t(pack_table, returned.reshape(slots, col_count))


def shards(
    face_len,
    residual,
    prev_direction,
    prev_rho,
    schur,
    neumann,
    coarse_basis,
    coarse_inverse,
    prim_owner,
    coarse_row,
):
    row_count = residual.shape[3]
    col_count = residual.shape[4]
    face_rows = row_count // 6
    primal = coarse_basis.shape[4]
    owned_rows = coarse_inverse.shape[3]
    lengths = face_len.reshape(6)
    live_mask = (
        (lax.broadcasted_iota(jnp.int32, (6, face_rows), 1) < lengths[:, None])
        .astype(jnp.float32)
        .reshape(row_count, 1)
    )
    residual_live = live_mask * residual.reshape(row_count, col_count)
    weighted = 0.5 * residual_live
    local_part = product(neumann.reshape(row_count, row_count), weighted)
    basis = coarse_basis.reshape(row_count, primal)
    coarse_terms = product_t(basis, weighted)
    correction = coarse_level(
        coarse_terms,
        prim_owner.reshape(primal),
        coarse_row.reshape(primal),
        coarse_inverse.reshape(owned_rows, owned_rows),
    )
    precond_image = local_part + product(basis, correction)
    precond = 0.5 * assemble(precond_image, live_mask)
    devices = lax.axis_size(("blk", "lat", "depth"))
    norm_scale = 0.5 / (devices * row_count)
    rho_now = norm_scale * lax.psum(
        jnp.sum(residual_live * precond, axis=0), ("blk", "lat", "depth")
    )
    direction = precond + rho_now / prev_rho * (
        live_mask * prev_direction.reshape(row_count, col_count)
    )
    schur_image = product(schur.reshape(row_count, row_count), direction)
    applied = assemble(schur_image, live_mask)
    curv_sum = lax.psum(jnp.sum(direction * applied, axis=0), ("blk", "lat", "depth"))
    step_alpha = rho_now / (norm_scale * curv_sum)
    new_residual = residual_live - step_alpha * applied
    res_norm = norm_scale * lax.psum(
        jnp.sum(new_residual * new_residual, axis=0), ("blk", "lat", "depth")
    )
    out_shape = (1, 1, 1, row_count, col_count)
    return (
        new_residual.reshape(out_shape),
        direction.reshape(out_shape),
        rho_now,
        step_alpha,
        res_norm,
    )


def solution(mesh):
    in_specs = (
        P("blk", "lat", "depth", None),
        P("blk", "lat", "depth", None, None),
        P("blk", "lat", "depth", None, None),
        P(),
        P("blk", "lat", "depth", None, None),
        P("blk", "lat", "depth", None, None),
        P("blk", "lat", "depth", None, None),
        P("blk", "lat", "depth", None, None),
        P("blk", "lat", "depth", None, None),
        P("blk", "lat", "depth", None),
    )
    out_specs = (
        P("blk", "lat", "depth", None, None),
        P("blk", "lat", "depth", None, None),
        P(),
        P(),
        P(),
    )
    return jax.shard_map(shards, mesh=mesh, in_specs=in_specs, out_specs=out_specs, check_vma=False)
```

profile of v0, /device:TPU:1, one launch (start us, length us, event | category | flops | bytes accessed | tf_op | source)
XLA Modules:
  0.0 437.7 jit_solution(7040188213010964891)
XLA Ops:
  0.6 0.8 fusion.32
  2.3 0.8 fusion.31
  3.1 0.7 add_add_fusion
  3.7 0.7 broadcast_add_fusion.1
  4.6 0.7 sub.15
  5.3 11.9 %all-to-all-start = ((s32[32,1,24]{2,1,0:T(1,128)}), s32[32,1,24]{2,1,0:T(1,128)S(1)}, u32[]{:S(2)}, u32[]{:S(2)}) async-start(s32[32,1,24]{2,1,0:T(1,128)} %bitcast.9), calls=%async_computation | async-start | bytes 32768 | tf_op jit(solution)/shard_map/all_to_all | solution.py:65
  17.2 0.7 convert_bitcast_fusion
  17.9 4.4 %fusion.6 = f32[512,256]{1,0:T(8,128)S(1)} fusion(f32[1,1,1,768,512]{4,3,2,1,0:T(8,128)} %param.11, f32[1,1,1,768,256]{4,3,2,1,0:T(8,128)} %param.16, f32[768]{0:T(1024)S(1)} %convert_bitcast_fusion), kind=kOutput, calls=%fused_computation.7 | convolution fusion | flops 1208745984 | bytes 2886656 | tf_op jit(solution)/shard_map/dot_general | solution.py:26
  22.3 2.0 fusion.17
  24.3 1.4 all-to-all-done
  25.7 7.9 %all-to-all-start.1 = ((f32[32,24,512]{2,1,0:T(8,128)}), f32[32,24,512]{2,1,0:T(8,128)}, u32[]{:S(2)}, u32[]{:S(2)}) async-start(f32[32,24,512]{2,1,0:T(8,128)} %bitcast.103), calls=%async_computation.1 | async-start | bytes 3145728 | tf_op jit(solution)/shard_map/all_to_all | solution.py:64
  34.1 0.7 reduce.5
  34.9 35.1 %all-to-all-done.1 = f32[32,24,512]{2,1,0:T(8,128)} async-done(((f32[32,24,512]{2,1,0:T(8,128)}), f32[32,24,512]{2,1,0:T(8,128)}, u32[]{:S(2)}, u32[]{:S(2)}) %all-to-all-start.1) | async-done | bytes 1572896 | tf_op jit(solution)/shard_map/all_to_all | solution.py:64
  70.1 2.4 fusion.15
  72.5 1.0 fusion.28
  73.5 2.1 fusion.22
  75.6 7.3 %all-to-all-start.2 = ((f32[32,24,512]{2,1,0:T(8,128)}), f32[32,24,512]{2,1,0:T(8,128)}, u32[]{:S(2)}, u32[]{:S(2)}) async-start(f32[32,24,512]{2,1,0:T(8,128)} %bitcast.100), calls=%async_computation.2 | async-start | bytes 3145728 | tf_op jit(solution)/shard_map/all_to_all | solution.py:74
  82.9 10.3 %fusion.2 = f32[512,768]{1,0:T(8,128)} fusion(f32[1,1,1,768,768]{4,3,2,1,0:T(8,128)S(1)} %copy-done, f32[1,1,1,768,512]{4,3,2,1,0:T(8,128)} %param.11, f32[768]{0:T(1024)S(1)} %convert_bitcast_fusion), kind=kOutput, calls=%fused_computation.2 | convolution fusion | flops 3624665088 | bytes 5508096 | tf_op jit(solution)/shard_map/dot_general | solution.py:22
  93.2 25.3 %all-to-all-done.2 = f32[32,24,512]{2,1,0:T(8,128)} async-done(((f32[32,24,512]{2,1,0:T(8,128)}), f32[32,24,512]{2,1,0:T(8,128)}, u32[]{:S(2)}, u32[]{:S(2)}) %all-to-all-start.2) | async-done | bytes 1572896 | tf_op jit(solution)/shard_map/all_to_all | solution.py:74
  118.5 2.5 fusion.16
  121.1 2.6 add_bitcast_fusion
  123.7 1.0 fusion.37
  125.0 0.7 collective-permute-start
  125.8 2.0 collective-permute-start.1
  127.7 3.0 copy.40
  130.7 3.0 copy.45
  133.8 5.3 %collective-permute-start.2 = (f32[128,512]{0,1:T(8,128)S(1)}, f32[128,512]{0,1:T(8,128)S(1)}, u32[]{:S(2)}, u32[]{:S(2)}) collective-permute-start(f32[128,512]{0,1:T(8,128)S(1)} %get-tuple-element.38), channel_id=1, source_target_pairs={{0,8},{8,16},{16,24},{1,9},{9,17},{17,25},{2,10},{10,18},{18,26},{... | collective-permute-start | bytes 786440 | tf_op jit(solution)/shard_map/ppermute | solution.py:18
  139.1 1.3 collective-permute-start.3
  140.4 5.9 %collective-permute-start.4 = (f32[128,512]{0,1:T(8,128)S(1)}, f32[128,512]{0,1:T(8,128)S(1)}, u32[]{:S(2)}, u32[]{:S(2)}) collective-permute-start(f32[128,512]{0,1:T(8,128)S(1)} %get-tuple-element.36), channel_id=1, source_target_pairs={{0,1},{1,2},{2,3},{3,4},{4,5},{5,6},{6,7},{8,9},{9,10},{10,11},{11... | collective-permute-start | bytes 786440 | tf_op jit(solution)/shard_map/ppermute | solution.py:18
  146.4 1.9 collective-permute-start.5
  148.3 1.7 bitcast_dynamic-update-slice_fusion.11
  150.0 1.7 bitcast_dynamic-update-slice_fusion.10
  151.6 0.7 bitcast_dynamic-update-slice_fusion.9
  152.4 0.7 bitcast_dynamic-update-slice_fusion.8
  153.1 0.7 bitcast_dynamic-update-slice_fusion.7
  154.0 0.7 bitcast_dynamic-update-slice_fusion.6
  154.8 3.0 copy.43
  157.8 3.0 copy.44
  160.8 2.7 multiply_reduce_fusion.2
  163.6 75.6 %psum.21 = f32[512]{0:T(512)S(1)} all-reduce(f32[512]{0:T(512)S(1)} %multiply_reduce_fusion.2), channel_id=1, replica_groups=mesh['blk'=8,'lat'=4,'depth'=8] {'blk','lat','depth'}, use_global_device_ids=true, to_apply=%region_5.6 | all-reduce | flops 512 | bytes 4096 | tf_op jit(solution)/shard_map/psum | solution.py:122
  239.2 2.9 fusion.5
  242.3 4.0 fusion.9
  246.4 1.0 fusion.36
  247.7 1.8 collective-permute-start.6
  249.5 0.9 collective-permute-start.7
  250.4 2.9 collective-permute-start.8
  253.3 1.3 collective-permute-start.9
  254.6 2.6 collective-permute-start.10
  257.2 3.0 copy.49
  260.2 3.0 collective-permute-start.11
  263.3 1.7 bitcast_dynamic-update-slice_fusion.5
  265.0 1.7 bitcast_dynamic-update-slice_fusion.4
  266.7 1.7 bitcast_dynamic-update-slice_fusion.3
  268.3 1.7 bitcast_dynamic-update-slice_fusion.2
  270.0 1.7 bitcast_dynamic-update-slice_fusion.1
  271.7 0.7 bitcast_dynamic-update-slice_fusion
  272.4 3.1 copy.46
  275.4 3.0 copy.47
  278.5 2.6 multiply_reduce_fusion.1
  281.1 74.9 %psum.22 = f32[512]{0:T(512)S(1)} all-reduce(f32[512]{0:T(512)S(1)} %multiply_reduce_fusion.1), channel_id=1, replica_groups=mesh['blk'=8,'lat'=4,'depth'=8] {'blk','lat','depth'}, use_global_device_ids=true, to_apply=%region_7.8 | all-reduce | flops 512 | bytes 4096 | tf_op jit(solution)/shard_map/psum | solution.py:130
  356.0 3.9 multiply_reduce_fusion
  359.9 3.0 copy.48
  362.9 74.2 %psum.23 = f32[512]{0:T(512)S(1)} all-reduce(f32[512]{0:T(512)S(1)} %get-tuple-element.25), channel_id=1, replica_groups=mesh['blk'=8,'lat'=4,'depth'=8] {'blk','lat','depth'}, use_global_device_ids=true, to_apply=%region_9.10 | all-reduce | flops 512 | bytes 4096 | tf_op jit(solution)/shard_map/psum | solution.py:133
  437.1 0.6 broadcast_multiply_fusion
  (44 shorter events, 2.7 us)
Async XLA Ops:
  0.6 82.2 %copy-start = (f32[1,1,1,768,768]{4,3,2,1,0:T(8,128)S(1)}, f32[1,1,1,768,768]{4,3,2,1,0:T(8,128)}, u32[]{:S(2)}) copy-start(f32[1,1,1,768,768]{4,3,2,1,0:T(8,128)} %param.15) | copy-start | bytes 7077892
  5.3 20.4 %all-to-all-start = ((s32[32,1,24]{2,1,0:T(1,128)}), s32[32,1,24]{2,1,0:T(1,128)S(1)}, u32[]{:S(2)}, u32[]{:S(2)}) async-start(s32[32,1,24]{2,1,0:T(1,128)} %bitcast.9), calls=%async_computation | async-start | bytes 32768 | tf_op jit(solution)/shard_map/all_to_all | solution.py:65
  25.7 44.4 %all-to-all-start.1 = ((f32[32,24,512]{2,1,0:T(8,128)}), f32[32,24,512]{2,1,0:T(8,128)}, u32[]{:S(2)}, u32[]{:S(2)}) async-start(f32[32,24,512]{2,1,0:T(8,128)} %bitcast.103), calls=%async_computation.1 | async-start | bytes 3145728 | tf_op jit(solution)/shard_map/all_to_all | solution.py:64
  33.6 38.8 %copy-start.7 = (f32[1,1,1,256,256]{4,3,2,1,0:T(8,128)S(1)}, f32[1,1,1,256,256]{4,3,2,1,0:T(8,128)}, u32[]{:S(2)}) copy-start(f32[1,1,1,256,256]{4,3,2,1,0:T(8,128)} %param.17) | copy-start | bytes 786436
  75.6 42.9 %all-to-all-start.2 = ((f32[32,24,512]{2,1,0:T(8,128)}), f32[32,24,512]{2,1,0:T(8,128)}, u32[]{:S(2)}, u32[]{:S(2)}) async-start(f32[32,24,512]{2,1,0:T(8,128)} %bitcast.100), calls=%async_computation.2 | async-start | bytes 3145728 | tf_op jit(solution)/shard_map/all_to_all | solution.py:74
  82.9 38.2 %copy-start.5 = (f32[1,1,1,768,256]{4,3,2,1,0:T(8,128)S(1)}, f32[1,1,1,768,256]{4,3,2,1,0:T(8,128)}, u32[]{:S(2)}) copy-start(f32[1,1,1,768,256]{4,3,2,1,0:T(8,128)} %param.16) | copy-start | bytes 2359300
  118.5 2.6 copy-start.4
  123.7 1.3 copy-start.2
  125.0 21.3 %collective-permute-start = (f32[128,512]{0,1:T(8,128)}, f32[128,512]{0,1:T(8,128)}, u32[]{:S(2)}, u32[]{:S(2)}) collective-permute-start(f32[128,512]{0,1:T(8,128)} %get-tuple-element.40), channel_id=1, source_target_pairs={{0,32},{32,64},{64,96},{96,128},{128,160},{160,192},{192,224},{224... | collective-permute-start | bytes 786440 | tf_op jit(solution)/shard_map/ppermute | solution.py:12
  125.8 24.2 %collective-permute-start.1 = (f32[128,512]{0,1:T(8,128)}, f32[128,512]{0,1:T(8,128)}, u32[]{:S(2)}, u32[]{:S(2)}) collective-permute-start(f32[128,512]{0,1:T(8,128)} %get-tuple-element.39), channel_id=1, source_target_pairs={{0,224},{32,0},{64,32},{96,64},{128,96},{160,128},{192,160},{224,1... | collective-permute-start | bytes 786440 | tf_op jit(solution)/shard_map/ppermute | solution.py:12
  133.8 17.9 %collective-permute-start.2 = (f32[128,512]{0,1:T(8,128)S(1)}, f32[128,512]{0,1:T(8,128)S(1)}, u32[]{:S(2)}, u32[]{:S(2)}) collective-permute-start(f32[128,512]{0,1:T(8,128)S(1)} %get-tuple-element.38), channel_id=1, source_target_pairs={{0,8},{8,16},{16,24},{1,9},{9,17},{17,25},{2,10},{10,18},{18,26},{... | collective-permute-start | bytes 786440 | tf_op jit(solution)/shard_map/ppermute | solution.py:18
  139.1 13.3 %collective-permute-start.3 = (f32[128,512]{0,1:T(8,128)S(1)}, f32[128,512]{0,1:T(8,128)S(1)}, u32[]{:S(2)}, u32[]{:S(2)}) collective-permute-start(f32[128,512]{0,1:T(8,128)S(1)} %get-tuple-element.37), channel_id=1, source_target_pairs={{8,0},{16,8},{24,16},{9,1},{17,9},{25,17},{10,2},{18,10},{26,18},{... | collective-permute-start | bytes 786440 | tf_op jit(solution)/shard_map/ppermute | solution.py:18
  140.4 12.7 %collective-permute-start.4 = (f32[128,512]{0,1:T(8,128)S(1)}, f32[128,512]{0,1:T(8,128)S(1)}, u32[]{:S(2)}, u32[]{:S(2)}) collective-permute-start(f32[128,512]{0,1:T(8,128)S(1)} %get-tuple-element.36), channel_id=1, source_target_pairs={{0,1},{1,2},{2,3},{3,4},{4,5},{5,6},{6,7},{8,9},{9,10},{10,11},{11... | collective-permute-start | bytes 786440 | tf_op jit(solution)/shard_map/ppermute | solution.py:18
  146.4 7.7 %collective-permute-start.5 = (f32[128,512]{0,1:T(8,128)S(1)}, f32[128,512]{0,1:T(8,128)S(1)}, u32[]{:S(2)}, u32[]{:S(2)}) collective-permute-start(f32[128,512]{0,1:T(8,128)S(1)} %get-tuple-element.35), channel_id=1, source_target_pairs={{1,0},{2,1},{3,2},{4,3},{5,4},{6,5},{7,6},{9,8},{10,9},{11,10},{12... | collective-permute-start | bytes 786440 | tf_op jit(solution)/shard_map/ppermute | solution.py:18
  160.8 78.4 %copy-start.10 = (f32[512]{0:T(512)S(1)}, f32[512]{0:T(512)}, u32[]{:S(2)}) copy-start(f32[512]{0:T(512)} %param.13) | copy-start | bytes 6148
  239.2 116.8 %copy-start.9 = (f32[512]{0:T(512)}, f32[512]{0:T(512)S(1)}, u32[]{:S(2)}) copy-start(f32[512]{0:T(512)S(1)} %get-tuple-element.28) | copy-start | bytes 6148
  239.2 3.1 copy-start.6
  242.3 4.1 copy-start.3
  246.4 1.3 copy-start.1
  247.7 12.6 %collective-permute-start.6 = (f32[128,512]{0,1:T(8,128)}, f32[128,512]{0,1:T(8,128)}, u32[]{:S(2)}, u32[]{:S(2)}) collective-permute-start(f32[128,512]{0,1:T(8,128)} %get-tuple-element.34), channel_id=1, source_target_pairs={{0,32},{32,64},{64,96},{96,128},{128,160},{160,192},{192,224},{224... | collective-permute-start | bytes 786440 | tf_op jit(solution)/shard_map/ppermute | solution.py:12
  249.5 15.5 %collective-permute-start.7 = (f32[128,512]{0,1:T(8,128)}, f32[128,512]{0,1:T(8,128)}, u32[]{:S(2)}, u32[]{:S(2)}) collective-permute-start(f32[128,512]{0,1:T(8,128)} %get-tuple-element.33), channel_id=1, source_target_pairs={{0,224},{32,0},{64,32},{96,64},{128,96},{160,128},{192,160},{224,1... | collective-permute-start | bytes 786440 | tf_op jit(solution)/shard_map/ppermute | solution.py:12
  250.4 16.3 %collective-permute-start.8 = (f32[128,512]{0,1:T(8,128)S(1)}, f32[128,512]{0,1:T(8,128)}, u32[]{:S(2)}, u32[]{:S(2)}) collective-permute-start(f32[128,512]{0,1:T(8,128)S(1)} %get-tuple-element.32), channel_id=1, source_target_pairs={{0,8},{8,16},{16,24},{1,9},{9,17},{17,25},{2,10},{10,18},{18,26},{... | collective-permute-start | bytes 786440 | tf_op jit(solution)/shard_map/ppermute | solution.py:18
  253.3 15.0 %collective-permute-start.9 = (f32[128,512]{0,1:T(8,128)S(1)}, f32[128,512]{0,1:T(8,128)}, u32[]{:S(2)}, u32[]{:S(2)}) collective-permute-start(f32[128,512]{0,1:T(8,128)S(1)} %get-tuple-element.31), channel_id=1, source_target_pairs={{8,0},{16,8},{24,16},{9,1},{17,9},{25,17},{10,2},{18,10},{26,18},{... | collective-permute-start | bytes 786440 | tf_op jit(solution)/shard_map/ppermute | solution.py:18
  254.6 15.4 %collective-permute-start.10 = (f32[128,512]{0,1:T(8,128)S(1)}, f32[128,512]{0,1:T(8,128)}, u32[]{:S(2)}, u32[]{:S(2)}) collective-permute-start(f32[128,512]{0,1:T(8,128)S(1)} %get-tuple-element.30), channel_id=1, source_target_pairs={{0,1},{1,2},{2,3},{3,4},{4,5},{5,6},{6,7},{8,9},{9,10},{10,11},{11... | collective-permute-start | bytes 786440 | tf_op jit(solution)/shard_map/ppermute | solution.py:18
  260.2 11.4 %collective-permute-start.11 = (f32[128,512]{0,1:T(8,128)S(1)}, f32[128,512]{0,1:T(8,128)S(1)}, u32[]{:S(2)}, u32[]{:S(2)}) collective-permute-start(f32[128,512]{0,1:T(8,128)S(1)} %get-tuple-element.29), channel_id=1, source_target_pairs={{1,0},{2,1},{3,2},{4,3},{5,4},{6,5},{7,6},{9,8},{10,9},{11,10},{12... | collective-permute-start | bytes 786440 | tf_op jit(solution)/shard_map/ppermute | solution.py:18
  356.0 3.9 copy-start.8
where the time goes:
time: 439 us; the launch traced here: 438 us
  blocking collectives  225 us (51%)
  waiting for transfers between devices  62.1 us (14%)
  starting transfers between devices  56.7 us (13%)
  local copies, waits for them, and re-layouts  43.9 us (10%)
  matrix products  31.4 us (7%)
  other arithmetic  18 us (4%)
    psum x1, blocking collectives, shards(): lax.psum(jnp.sum(residual_live * precond, axis=0), ('blk', 'lat', 'depth'))  75.6 us
    psum x1, blocking collectives, shards(): lax.psum(jnp.sum(direction * applied, axis=0), ('blk', 'lat', 'depth'))  74.9 us
    psum x1, blocking collectives, shards(): lax.psum(jnp.sum(new_residual * new_residual, axis=0), ('blk', 'lat', 'de...  74.2 us
    all_to_all x1, waiting for transfers between devices, coarse_level(): lax.all_to_all(outgoing, ('blk', 'lat'), split_axis=0, concat_axis=0, til...  35.1 us
    unnamed x36, local copies, waits for them, and re-layouts  26.8 us
    all_to_all x1, waiting for transfers between devices, coarse_level(): lax.all_to_all(answers.reshape(owners, CAP, col_count), ('blk', 'lat'), s...  25.3 us
    ppermute x8, starting transfers between devices, passed_along(): return lax.ppermute(block, axis, route)  24.4 us
    dot_general x6, matrix products, product(): jnp.dot(left, right, precision=exact_mode, preferred_element_type=jnp.flo...  22.3 us
  transfers between devices with their start and end apart: 15, of which 4 were waited for; matrix products, arithmetic and copies ran while one was open for 10% of the time, Pallas kernels for 0%

commit v1 on v0

--- a/solution.py
+++ b/solution.py
@@ -127,7 +127,9 @@
     )
     schur_image = product(schur.reshape(row_count, row_count), direction)
     applied = assemble(schur_image, live_mask)
-    curv_sum = lax.psum(jnp.sum(direction * applied, axis=0), ("blk", "lat", "depth"))
+    curv_sum = jnp.sum(
+        lax.all_gather(jnp.sum(direction * applied, axis=0), ("blk", "lat", "depth")), axis=0
+    )
     step_alpha = rho_now / (norm_scale * curv_sum)
     new_residual = residual_live - step_alpha * applied
     res_norm = norm_scale * lax.psum(

time: 439 us -> 439 us (level); the launches traced: 438 us -> 431 us
  blocking collectives: 225 us -> 217 us
    psum x1 -> x0, blocking collectives: 74.9 us -> none  [shards(): lax.psum(jnp.sum(direction * applied, axis=0), ('blk', 'lat', 'depth'))]
    all_gather x0 -> x1, blocking collectives: none -> 68 us  [shards(): lax.all_gather(jnp.sum(direction * applied, axis=0), ('blk', 'lat', 'dept...]
where the time goes in v1:
time: 439 us; the launch traced here: 431 us
  blocking collectives  217 us (49%)
  waiting for transfers between devices  62.3 us (14%)
  starting transfers between devices  57.2 us (13%)
  local copies, waits for them, and re-layouts  43.9 us (10%)
  matrix products  31.4 us (7%)
  other arithmetic  18.3 us (4%)
    psum x1, blocking collectives, shards(): lax.psum(jnp.sum(residual_live * precond, axis=0), ('blk', 'lat', 'depth'))  75.6 us
    psum x1, blocking collectives, shards(): lax.psum(jnp.sum(new_residual * new_residual, axis=0), ('blk', 'lat', 'de...  73.3 us
    all_gather x1, blocking collectives, shards(): lax.all_gather(jnp.sum(direction * applied, axis=0), ('blk', 'lat', 'dept...  68 us
    all_to_all x1, waiting for transfers between devices, coarse_level(): lax.all_to_all(outgoing, ('blk', 'lat'), split_axis=0, concat_axis=0, til...  35.1 us
    unnamed x36, local copies, waits for them, and re-layouts  26.8 us
    all_to_all x1, waiting for transfers between devices, coarse_level(): lax.all_to_all(answers.reshape(owners, CAP, col_count), ('blk', 'lat'), s...  25.5 us
    ppermute x8, starting transfers between devices, passed_along(): return lax.ppermute(block, axis, route)  24.3 us
    dot_general x6, matrix products, product(): jnp.dot(left, right, precision=exact_mode, preferred_element_type=jnp.flo...  22.3 us
  transfers between devices with their start and end apart: 15, of which 4 were waited for; matrix products, arithmetic and copies ran while one was open for 10% of the time, Pallas kernels for 0%

profile of v1, /device:TPU:1, one launch (start us, length us, event | category | flops | bytes accessed | tf_op | source)
XLA Modules:
  0.0 431.1 jit_solution(1173386846563768257)
XLA Ops:
  0.6 0.8 fusion.32
  2.3 0.8 fusion.31
  3.1 0.7 add_add_fusion
  3.7 0.7 broadcast_add_fusion.1
  4.6 0.7 sub.15
  5.3 11.9 %all-to-all-start = ((s32[32,1,24]{2,1,0:T(1,128)}), s32[32,1,24]{2,1,0:T(1,128)S(1)}, u32[]{:S(2)}, u32[]{:S(2)}) async-start(s32[32,1,24]{2,1,0:T(1,128)} %bitcast.9), calls=%async_computation | async-start | bytes 32768 | tf_op jit(solution)/shard_map/all_to_all | solution.py:65
  17.2 0.7 convert_bitcast_fusion
  17.9 4.4 %fusion.6 = f32[512,256]{1,0:T(8,128)S(1)} fusion(f32[1,1,1,768,512]{4,3,2,1,0:T(8,128)} %param.11, f32[1,1,1,768,256]{4,3,2,1,0:T(8,128)} %param.16, f32[768]{0:T(1024)S(1)} %convert_bitcast_fusion), kind=kOutput, calls=%fused_computation.7 | convolution fusion | flops 1208745984 | bytes 2886656 | tf_op jit(solution)/shard_map/dot_general | solution.py:26
  22.3 2.0 fusion.17
  24.3 1.4 all-to-all-done
  25.7 7.9 %all-to-all-start.1 = ((f32[32,24,512]{2,1,0:T(8,128)}), f32[32,24,512]{2,1,0:T(8,128)}, u32[]{:S(2)}, u32[]{:S(2)}) async-start(f32[32,24,512]{2,1,0:T(8,128)} %bitcast.104), calls=%async_computation.1 | async-start | bytes 3145728 | tf_op jit(solution)/shard_map/all_to_all | solution.py:64
  34.1 0.7 reduce.6
  34.9 35.1 %all-to-all-done.1 = f32[32,24,512]{2,1,0:T(8,128)} async-done(((f32[32,24,512]{2,1,0:T(8,128)}), f32[32,24,512]{2,1,0:T(8,128)}, u32[]{:S(2)}, u32[]{:S(2)}) %all-to-all-start.1) | async-done | bytes 1572896 | tf_op jit(solution)/shard_map/all_to_all | solution.py:64
  70.1 2.4 fusion.15
  72.5 1.0 fusion.28
  73.5 2.1 fusion.22
  75.6 7.6 %all-to-all-start.2 = ((f32[32,24,512]{2,1,0:T(8,128)}), f32[32,24,512]{2,1,0:T(8,128)}, u32[]{:S(2)}, u32[]{:S(2)}) async-start(f32[32,24,512]{2,1,0:T(8,128)} %bitcast.101), calls=%async_computation.2 | async-start | bytes 3145728 | tf_op jit(solution)/shard_map/all_to_all | solution.py:74
  83.2 10.3 %fusion.2 = f32[512,768]{1,0:T(8,128)} fusion(f32[1,1,1,768,768]{4,3,2,1,0:T(8,128)S(1)} %copy-done, f32[1,1,1,768,512]{4,3,2,1,0:T(8,128)} %param.11, f32[768]{0:T(1024)S(1)} %convert_bitcast_fusion), kind=kOutput, calls=%fused_computation.2 | convolution fusion | flops 3624665088 | bytes 5508096 | tf_op jit(solution)/shard_map/dot_general | solution.py:22
  93.5 25.5 %all-to-all-done.2 = f32[32,24,512]{2,1,0:T(8,128)} async-done(((f32[32,24,512]{2,1,0:T(8,128)}), f32[32,24,512]{2,1,0:T(8,128)}, u32[]{:S(2)}, u32[]{:S(2)}) %all-to-all-start.2) | async-done | bytes 1572896 | tf_op jit(solution)/shard_map/all_to_all | solution.py:74
  118.9 2.5 fusion.16
  121.5 2.6 add_bitcast_fusion
  124.1 1.0 fusion.37
  125.5 0.8 collective-permute-start
  126.3 2.0 collective-permute-start.1
  128.3 3.0 copy.40
  131.3 3.0 copy.45
  134.3 5.4 %collective-permute-start.2 = (f32[128,512]{0,1:T(8,128)S(1)}, f32[128,512]{0,1:T(8,128)S(1)}, u32[]{:S(2)}, u32[]{:S(2)}) collective-permute-start(f32[128,512]{0,1:T(8,128)S(1)} %get-tuple-element.38), channel_id=1, source_target_pairs={{0,8},{8,16},{16,24},{1,9},{9,17},{17,25},{2,10},{10,18},{18,26},{... | collective-permute-start | bytes 786440 | tf_op jit(solution)/shard_map/ppermute | solution.py:18
  139.7 1.3 collective-permute-start.3
  141.0 5.9 %collective-permute-start.4 = (f32[128,512]{0,1:T(8,128)S(1)}, f32[128,512]{0,1:T(8,128)S(1)}, u32[]{:S(2)}, u32[]{:S(2)}) collective-permute-start(f32[128,512]{0,1:T(8,128)S(1)} %get-tuple-element.36), channel_id=1, source_target_pairs={{0,1},{1,2},{2,3},{3,4},{4,5},{5,6},{6,7},{8,9},{9,10},{10,11},{11... | collective-permute-start | bytes 786440 | tf_op jit(solution)/shard_map/ppermute | solution.py:18
  147.0 1.9 collective-permute-start.5
  148.9 1.7 bitcast_dynamic-update-slice_fusion.11
  150.6 1.7 bitcast_dynamic-update-slice_fusion.10
  152.2 0.7 bitcast_dynamic-update-slice_fusion.9
  153.0 0.7 bitcast_dynamic-update-slice_fusion.8
  153.7 0.7 bitcast_dynamic-update-slice_fusion.7
  154.7 0.7 bitcast_dynamic-update-slice_fusion.6
  155.4 3.0 copy.43
  158.4 3.0 copy.44
  161.4 2.7 multiply_reduce_fusion.2
  164.2 75.6 %psum.14 = f32[512]{0:T(512)S(1)} all-reduce(f32[512]{0:T(512)S(1)} %multiply_reduce_fusion.2), channel_id=1, replica_groups=mesh['blk'=8,'lat'=4,'depth'=8] {'blk','lat','depth'}, use_global_device_ids=true, to_apply=%region_5.6 | all-reduce | flops 512 | bytes 4096 | tf_op jit(solution)/shard_map/psum | solution.py:122
  239.8 2.9 fusion.5
  242.9 4.0 fusion.9
  247.0 1.0 fusion.36
  248.3 1.8 collective-permute-start.6
  250.1 0.9 collective-permute-start.7
  251.0 2.9 collective-permute-start.8
  253.9 1.3 collective-permute-start.9
  255.2 2.6 collective-permute-start.10
  257.8 3.0 copy.49
  260.9 3.0 collective-permute-start.11
  263.9 1.7 bitcast_dynamic-update-slice_fusion.5
  265.6 1.7 bitcast_dynamic-update-slice_fusion.4
  267.2 1.7 bitcast_dynamic-update-slice_fusion.3
  268.9 1.7 bitcast_dynamic-update-slice_fusion.2
  270.6 1.7 bitcast_dynamic-update-slice_fusion.1
  272.2 0.7 bitcast_dynamic-update-slice_fusion
  273.0 3.1 copy.46
  276.0 3.0 copy.47
  279.0 2.6 multiply_reduce_fusion.1
  281.7 68.0 %all-gather.1 = f32[256,1,512]{2,1,0:T(1,128)S(1)} all-gather(f32[1,1,512]{2,1,0:T(1,128)S(1)} %bitcast.109), channel_id=2, replica_groups=mesh['blk'=8,'lat'=4,'depth'=8] {'blk','lat','depth'}, dimensions={0}, use_global_device_ids=true | all-gather | bytes 526336 | tf_op jit(solution)/shard_map/all_gather | solution.py:131
  350.1 3.9 multiply_reduce_fusion
  354.0 3.0 copy.48
  357.0 73.3 %psum.15 = f32[512]{0:T(512)S(1)} all-reduce(f32[512]{0:T(512)S(1)} %get-tuple-element.25), channel_id=1, replica_groups=mesh['blk'=8,'lat'=4,'depth'=8] {'blk','lat','depth'}, use_global_device_ids=true, to_apply=%region_9.10 | all-reduce | flops 512 | bytes 4096 | tf_op jit(solution)/shard_map/psum | solution.py:135
  430.3 0.6 broadcast_multiply_fusion
  (45 shorter events, 3.0 us)
Async XLA Ops:
  0.6 82.5 %copy-start = (f32[1,1,1,768,768]{4,3,2,1,0:T(8,128)S(1)}, f32[1,1,1,768,768]{4,3,2,1,0:T(8,128)}, u32[]{:S(2)}) copy-start(f32[1,1,1,768,768]{4,3,2,1,0:T(8,128)} %param.15) | copy-start | bytes 7077892
  5.3 20.4 %all-to-all-start = ((s32[32,1,24]{2,1,0:T(1,128)}), s32[32,1,24]{2,1,0:T(1,128)S(1)}, u32[]{:S(2)}, u32[]{:S(2)}) async-start(s32[32,1,24]{2,1,0:T(1,128)} %bitcast.9), calls=%async_computation | async-start | bytes 32768 | tf_op jit(solution)/shard_map/all_to_all | solution.py:65
  25.7 44.3 %all-to-all-start.1 = ((f32[32,24,512]{2,1,0:T(8,128)}), f32[32,24,512]{2,1,0:T(8,128)}, u32[]{:S(2)}, u32[]{:S(2)}) async-start(f32[32,24,512]{2,1,0:T(8,128)} %bitcast.104), calls=%async_computation.1 | async-start | bytes 3145728 | tf_op jit(solution)/shard_map/all_to_all | solution.py:64
  33.6 38.8 %copy-start.7 = (f32[1,1,1,256,256]{4,3,2,1,0:T(8,128)S(1)}, f32[1,1,1,256,256]{4,3,2,1,0:T(8,128)}, u32[]{:S(2)}) copy-start(f32[1,1,1,256,256]{4,3,2,1,0:T(8,128)} %param.17) | copy-start | bytes 786436
  75.6 43.4 %all-to-all-start.2 = ((f32[32,24,512]{2,1,0:T(8,128)}), f32[32,24,512]{2,1,0:T(8,128)}, u32[]{:S(2)}, u32[]{:S(2)}) async-start(f32[32,24,512]{2,1,0:T(8,128)} %bitcast.101), calls=%async_computation.2 | async-start | bytes 3145728 | tf_op jit(solution)/shard_map/all_to_all | solution.py:74
  83.2 38.3 %copy-start.5 = (f32[1,1,1,768,256]{4,3,2,1,0:T(8,128)S(1)}, f32[1,1,1,768,256]{4,3,2,1,0:T(8,128)}, u32[]{:S(2)}) copy-start(f32[1,1,1,768,256]{4,3,2,1,0:T(8,128)} %param.16) | copy-start | bytes 2359300
  118.9 2.6 copy-start.4
  124.1 1.3 copy-start.2
  125.5 21.5 %collective-permute-start = (f32[128,512]{0,1:T(8,128)}, f32[128,512]{0,1:T(8,128)}, u32[]{:S(2)}, u32[]{:S(2)}) collective-permute-start(f32[128,512]{0,1:T(8,128)} %get-tuple-element.40), channel_id=1, source_target_pairs={{0,32},{32,64},{64,96},{96,128},{128,160},{160,192},{192,224},{224... | collective-permute-start | bytes 786440 | tf_op jit(solution)/shard_map/ppermute | solution.py:12
  126.3 24.3 %collective-permute-start.1 = (f32[128,512]{0,1:T(8,128)}, f32[128,512]{0,1:T(8,128)}, u32[]{:S(2)}, u32[]{:S(2)}) collective-permute-start(f32[128,512]{0,1:T(8,128)} %get-tuple-element.39), channel_id=1, source_target_pairs={{0,224},{32,0},{64,32},{96,64},{128,96},{160,128},{192,160},{224,1... | collective-permute-start | bytes 786440 | tf_op jit(solution)/shard_map/ppermute | solution.py:12
  134.3 17.9 %collective-permute-start.2 = (f32[128,512]{0,1:T(8,128)S(1)}, f32[128,512]{0,1:T(8,128)S(1)}, u32[]{:S(2)}, u32[]{:S(2)}) collective-permute-start(f32[128,512]{0,1:T(8,128)S(1)} %get-tuple-element.38), channel_id=1, source_target_pairs={{0,8},{8,16},{16,24},{1,9},{9,17},{17,25},{2,10},{10,18},{18,26},{... | collective-permute-start | bytes 786440 | tf_op jit(solution)/shard_map/ppermute | solution.py:18
  139.7 13.3 %collective-permute-start.3 = (f32[128,512]{0,1:T(8,128)S(1)}, f32[128,512]{0,1:T(8,128)S(1)}, u32[]{:S(2)}, u32[]{:S(2)}) collective-permute-start(f32[128,512]{0,1:T(8,128)S(1)} %get-tuple-element.37), channel_id=1, source_target_pairs={{8,0},{16,8},{24,16},{9,1},{17,9},{25,17},{10,2},{18,10},{26,18},{... | collective-permute-start | bytes 786440 | tf_op jit(solution)/shard_map/ppermute | solution.py:18
  141.0 12.7 %collective-permute-start.4 = (f32[128,512]{0,1:T(8,128)S(1)}, f32[128,512]{0,1:T(8,128)S(1)}, u32[]{:S(2)}, u32[]{:S(2)}) collective-permute-start(f32[128,512]{0,1:T(8,128)S(1)} %get-tuple-element.36), channel_id=1, source_target_pairs={{0,1},{1,2},{2,3},{3,4},{4,5},{5,6},{6,7},{8,9},{9,10},{10,11},{11... | collective-permute-start | bytes 786440 | tf_op jit(solution)/shard_map/ppermute | solution.py:18
  147.0 7.7 %collective-permute-start.5 = (f32[128,512]{0,1:T(8,128)S(1)}, f32[128,512]{0,1:T(8,128)S(1)}, u32[]{:S(2)}, u32[]{:S(2)}) collective-permute-start(f32[128,512]{0,1:T(8,128)S(1)} %get-tuple-element.35), channel_id=1, source_target_pairs={{1,0},{2,1},{3,2},{4,3},{5,4},{6,5},{7,6},{9,8},{10,9},{11,10},{12... | collective-permute-start | bytes 786440 | tf_op jit(solution)/shard_map/ppermute | solution.py:18
  161.4 78.4 %copy-start.10 = (f32[512]{0:T(512)S(1)}, f32[512]{0:T(512)}, u32[]{:S(2)}) copy-start(f32[512]{0:T(512)} %param.13) | copy-start | bytes 6148
  239.8 110.2 %copy-start.9 = (f32[512]{0:T(512)}, f32[512]{0:T(512)S(1)}, u32[]{:S(2)}) copy-start(f32[512]{0:T(512)S(1)} %get-tuple-element.28) | copy-start | bytes 6148
  239.8 3.1 copy-start.6
  242.9 4.0 copy-start.3
  247.0 1.3 copy-start.1
  248.3 12.6 %collective-permute-start.6 = (f32[128,512]{0,1:T(8,128)}, f32[128,512]{0,1:T(8,128)}, u32[]{:S(2)}, u32[]{:S(2)}) collective-permute-start(f32[128,512]{0,1:T(8,128)} %get-tuple-element.34), channel_id=1, source_target_pairs={{0,32},{32,64},{64,96},{96,128},{128,160},{160,192},{192,224},{224... | collective-permute-start | bytes 786440 | tf_op jit(solution)/shard_map/ppermute | solution.py:12
  250.1 15.5 %collective-permute-start.7 = (f32[128,512]{0,1:T(8,128)}, f32[128,512]{0,1:T(8,128)}, u32[]{:S(2)}, u32[]{:S(2)}) collective-permute-start(f32[128,512]{0,1:T(8,128)} %get-tuple-element.33), channel_id=1, source_target_pairs={{0,224},{32,0},{64,32},{96,64},{128,96},{160,128},{192,160},{224,1... | collective-permute-start | bytes 786440 | tf_op jit(solution)/shard_map/ppermute | solution.py:12
  251.0 16.3 %collective-permute-start.8 = (f32[128,512]{0,1:T(8,128)S(1)}, f32[128,512]{0,1:T(8,128)}, u32[]{:S(2)}, u32[]{:S(2)}) collective-permute-start(f32[128,512]{0,1:T(8,128)S(1)} %get-tuple-element.32), channel_id=1, source_target_pairs={{0,8},{8,16},{16,24},{1,9},{9,17},{17,25},{2,10},{10,18},{18,26},{... | collective-permute-start | bytes 786440 | tf_op jit(solution)/shard_map/ppermute | solution.py:18
  253.9 15.0 %collective-permute-start.9 = (f32[128,512]{0,1:T(8,128)S(1)}, f32[128,512]{0,1:T(8,128)}, u32[]{:S(2)}, u32[]{:S(2)}) collective-permute-start(f32[128,512]{0,1:T(8,128)S(1)} %get-tuple-element.31), channel_id=1, source_target_pairs={{8,0},{16,8},{24,16},{9,1},{17,9},{25,17},{10,2},{18,10},{26,18},{... | collective-permute-start | bytes 786440 | tf_op jit(solution)/shard_map/ppermute | solution.py:18
  255.2 15.4 %collective-permute-start.10 = (f32[128,512]{0,1:T(8,128)S(1)}, f32[128,512]{0,1:T(8,128)}, u32[]{:S(2)}, u32[]{:S(2)}) collective-permute-start(f32[128,512]{0,1:T(8,128)S(1)} %get-tuple-element.30), channel_id=1, source_target_pairs={{0,1},{1,2},{2,3},{3,4},{4,5},{5,6},{6,7},{8,9},{9,10},{10,11},{11... | collective-permute-start | bytes 786440 | tf_op jit(solution)/shard_map/ppermute | solution.py:18
  260.9 11.4 %collective-permute-start.11 = (f32[128,512]{0,1:T(8,128)S(1)}, f32[128,512]{0,1:T(8,128)S(1)}, u32[]{:S(2)}, u32[]{:S(2)}) collective-permute-start(f32[128,512]{0,1:T(8,128)S(1)} %get-tuple-element.29), channel_id=1, source_target_pairs={{1,0},{2,1},{3,2},{4,3},{5,4},{6,5},{7,6},{9,8},{10,9},{11,10},{12... | collective-permute-start | bytes 786440 | tf_op jit(solution)/shard_map/ppermute | solution.py:18
  350.0 3.9 copy-start.8
